TPU v7x, 32 devices: a whole 2x2x4 slice. The times are simulated.
32 devices in a mesh: wide: 8 (over y, x, core), narrow: 4 (over z).
Axes of the slice: x: 2, y: 2, z: 4, core: 2. Of those that a mesh axis runs over, the one named last changes fastest.
Arguments:
- residual: bfloat16 [192, 16384], P(('wide', 'narrow')), may hold values from -10 to 10
- queries: bfloat16 [192, 16384], P(('wide', 'narrow')), may hold values from -10 to 10
- keys: bfloat16 [192, 8, 256, 128], P(('wide', 'narrow')), may hold values from -6 to 6
- values: bfloat16 [192, 8, 256, 128], P(('wide', 'narrow')), may hold values from -6 to 6
- cache_lengths: int32 [192], P(('wide', 'narrow')), may hold values from 2 to 256, as said below
- track_numbers: int32 [192], P(('wide', 'narrow')), may hold values from 0 to 15
- track_table: bfloat16 [16, 16384], replicated, may hold values from -3 to 3
- norm_gain: bfloat16 [16384], replicated, may hold values from 0.099609375 to 1.8984375
- gate_weight: bfloat16 [16384, 28672], P('narrow', 'wide'), may hold values from -0.046875 to 0.046875
- up_weight: bfloat16 [16384, 28672], P('narrow', 'wide'), may hold values from -0.046875 to 0.046875
- down_weight: bfloat16 [28672, 16384], P('wide', 'narrow'), may hold values from -0.046875 to 0.046875
Outputs:
- attended: bfloat16 [192, 16384], P(('wide', 'narrow'))
- ffn_out: bfloat16 [192, 16384], P(('wide', 'narrow'))
Inputs may be any that keep to these rules, and one draw needn't show every extreme that they name: `cache_lengths`: positions below a sequence's length hold its keys and values; some sequence fills all 256 positions.
All inputs are finite; a program needn't handle non-finite values.
Results may differ from a plain program's by a relative error of at most 0.0067.
Values may be sent and summed in bfloat16 or wider, within the bound.
A program may use at most 192 MiB of HBM per device.

v0:
```python
import math

import jax
import jax.numpy as jnp
from jax import lax
from jax.sharding import PartitionSpec as P


def per_device(
    residual,
    queries,
    keys,
    values,
    cache_lengths,
    track_numbers,
    track_table,
    norm_gain,
    gate_weight,
    up_weight,
    down_weight,
):
    batch_rows = residual.shape[0]
    key_heads = keys.shape[1]
    cache_size = keys.shape[2]
    head_size = keys.shape[3]
    grouped = queries.reshape(batch_rows, key_heads, -1, head_size)
    scores = jnp.einsum(
        "bkgd,bkld->bkgl", grouped, keys, preferred_element_type=jnp.float32
    ) / math.sqrt(head_size)
    visible = jnp.arange(cache_size, dtype=jnp.int32)[None, :] < cache_lengths[:, None]
    scores = jnp.where(visible[:, None, None, :], scores, -jnp.inf)
    highest = jnp.max(scores, axis=-1, keepdims=True)
    weights = jnp.exp(scores - highest)
    probs = (weights / jnp.sum(weights, axis=-1, keepdims=True)).astype(jnp.bfloat16)
    context = jnp.einsum(
        "bkgl,bkld->bkgd", probs, values, preferred_element_type=jnp.float32
    ).reshape(batch_rows, -1)
    one_hot = (
        track_numbers[:, None] == jnp.arange(track_table.shape[0], dtype=jnp.int32)[None, :]
    ).astype(jnp.bfloat16)
    stream = (
        residual.astype(jnp.float32)
        + context
        + jnp.dot(one_hot, track_table, preferred_element_type=jnp.float32)
    )
    attended = stream.astype(jnp.bfloat16)
    scale = lax.rsqrt(jnp.mean(stream * stream, axis=-1, keepdims=True) + 1e-05)
    normed = (stream * scale * norm_gain.astype(jnp.float32)).astype(jnp.bfloat16)
    columns = lax.all_to_all(normed, "narrow", split_axis=1, concat_axis=0, tiled=True)
    piece = lax.all_gather(columns, "wide", axis=0, tiled=True)
    partial_value = jnp.stack(
        [
            jnp.dot(piece, gate_weight, preferred_element_type=jnp.float32),
            jnp.dot(piece, up_weight, preferred_element_type=jnp.float32),
        ],
        0,
    )
    summed = lax.psum(partial_value, "narrow")
    hidden = (jax.nn.silu(summed[0]) * summed[1]).astype(jnp.bfloat16)
    wide_count = lax.axis_size("wide")
    narrow_count = lax.axis_size("narrow")
    term = jnp.dot(hidden, down_weight, preferred_element_type=jnp.float32)
    slices = lax.psum_scatter(term, "wide", scatter_dimension=1, tiled=True).astype(jnp.bfloat16)
    width_slice = slices.shape[1]
    arrived = lax.all_to_all(slices, ("wide", "narrow"), split_axis=0, concat_axis=1, tiled=True)
    ffn_out = (
        arrived.reshape(batch_rows, wide_count, narrow_count, width_slice)
        .transpose(0, 2, 1, 3)
        .reshape(batch_rows, -1)
    )
    return (attended, ffn_out)


def solution(mesh):
    in_specs = (
        P(("wide", "narrow"), None),
        P(("wide", "narrow"), None),
        P(("wide", "narrow"), None, None, None),
        P(("wide", "narrow"), None, None, None),
        P(("wide", "narrow")),
        P(("wide", "narrow")),
        P(),
        P(),
        P("narrow", "wide"),
        P("narrow", "wide"),
        P("wide", "narrow"),
    )
    out_specs = (P(("wide", "narrow"), None), P(("wide", "narrow"), None))
    return jax.shard_map(
        per_device, mesh=mesh, in_specs=in_specs, out_specs=out_specs, check_vma=False
    )
```

profile of v0, /device:TPU:0, one launch (start us, length us, event | category | flops | bytes accessed | tf_op | source)
XLA Modules:
  0.0 371.9 jit_solution(10993541123894389561)
XLA Ops:
  7.2 0.0 copy-start
  7.2 0.0 all-gather.2.cloned.1.call-start
  7.2 0.9 iota_compare_fusion
  8.1 0.8 convert_element_type.25
  8.9 1.0 copy.16
  9.9 0.0 copy-done
  9.9 0.9 fusion.8
  10.8 0.0 copy-start.2
  10.8 0.9 copy-done.2
  11.7 0.0 copy-start.3
  11.7 0.0 copy-start.4
  11.7 0.0 copy-start.5
  11.7 0.3 fusion.14
  12.0 3.8 %fusion.9 = f32[6,8,16,128]{3,2,1,0:T(8,128)S(1)} fusion(bf16[6,8,256,128]{3,2,1,0:T(8,128)(2,1)} %param.14, f32[6,8,16]{2,1,0:T(8,128)S(1)} %fusion.14, f32[6,8,16,256]{3,2,1,0:T(8,128)} %copy-done.2), kind=kOutput, calls=%fused_computation.19 | convolution fusion | flops 50922496 | bytes 4328448 | tf_op jit(solution)/shard_map/bkgl,bkld->bkgd/dot_general | solution.py:35
  15.8 0.0 copy-done.3
  15.8 0.0 copy-done.4
  15.8 0.0 copy-done.5
  15.8 0.5 multiply_reduce_fusion
  16.4 0.8 multiply_convert_fusion
  17.1 15.0 %all_to_all.35 = bf16[6,4,4096]{2,0,1:T(8,128)(2,1)S(1)} all-to-all(bf16[6,4,4096]{2,0,1:T(8,128)(2,1)S(1)} %bitcast.50), channel_id=1, replica_groups=mesh['wide'=8,'narrow'=4] {'narrow'}, dimensions={1} | all-to-all | bytes 393216 | tf_op jit(solution)/shard_map/all_to_all | solution.py:49
  32.1 0.7 all_to_all.29
  32.9 0.0 all-gather.2.cloned.1.call-update
  32.9 0.0 all-reduce.2.cloned.1.call-start
  32.9 24.8 %all-gather.2.cloned.1.call-done = bf16[192,4096]{1,0:T(8,128)(2,1)} async-done(((bf16[24,4096]{1,0:T(8,128)(2,1)}), bf16[192,4096]{1,0:T(8,128)(2,1)}) %all-gather.2.cloned.1.call-update) | async-done | bytes 1572880 | tf_op jit(solution)/shard_map/all_gather | solution.py:50
  57.7 0.0 copy-start.6
  57.7 15.9 %convolution_bitcast_fusion = f32[1,192,3584]{2,1,0:T(8,128)S(1)} fusion(bf16[192,4096]{1,0:T(8,128)(2,1)} %all-gather.2.cloned.1.call-done, bf16[4096,3584]{1,0:T(8,128)(2,1)} %param.20), kind=kOutput, calls=%fused_computation.3 | convolution fusion | flops 5637144576 | bytes 33685504 | tf_op jit(solution)/shard_map/dot_general | solution.py:54
  73.6 0.0 copy-done.6
  73.6 12.4 %convolution_bitcast_fusion.1 = f32[1,192,3584]{2,1,0:T(8,128)S(1)} fusion(bf16[192,4096]{1,0:T(8,128)(2,1)S(1)} %copy-done.6, bf16[4096,3584]{1,0:T(8,128)(2,1)} %param.19), kind=kOutput, calls=%fused_computation.4 | convolution fusion | flops 5637144576 | bytes 33685504 | tf_op jit(solution)/shard_map/dot_general | solution.py:53
  86.1 2.8 pad_maximum_fusion
  88.9 0.0 all-reduce.2.cloned.1.call-update
  88.9 0.0 reduce-scatter.2.cloned.1.call-start
  88.9 197.5 %all-reduce.2.cloned.1.call-done = f32[2,192,3584]{2,1,0:T(8,128)} async-done(((f32[2,192,3584]{2,1,0:T(8,128)}), f32[2,192,3584]{2,1,0:T(8,128)}) %all-reduce.2.cloned.1.call-update) | async-done | bytes 5505040 | tf_op jit(solution)/shard_map/psum | solution.py:58
  286.5 0.0 copy-start.1
  286.5 15.5 %fusion.4 = f32[192,4096]{1,0:T(8,128)} fusion(bf16[3584,4096]{1,0:T(8,128)(2,1)} %param.21, f32[2,192,3584]{2,1,0:T(8,128)} %all-reduce.2.cloned.1.call-done), kind=kOutput, calls=%fused_computation.10 | convolution fusion | flops 5641273344 | bytes 38010880 | tf_op jit(solution)/shard_map/dot_general | solution.py:62
  302.0 0.0 reduce-scatter.2.cloned.1.call-update
  302.0 45.1 %reduce-scatter.2.cloned.1.call-done = f32[192,512]{1,0:T(8,128)} async-done(((f32[192,4096]{1,0:T(8,128)}), f32[192,512]{1,0:T(8,128)}) %reduce-scatter.2.cloned.1.call-update) | async-done | bytes 393232 | tf_op jit(solution)/shard_map/reduce_scatter | solution.py:63
  347.1 1.7 convert_element_type.28
  348.8 1.0 all_to_all.30
  349.8 14.6 %all_to_all.36 = bf16[32,6,512]{2,1,0:T(8,128)(2,1)S(1)} all-to-all(bf16[32,6,512]{2,1,0:T(8,128)(2,1)S(1)} %all_to_all.30), channel_id=1, replica_groups=mesh['wide'=8,'narrow'=4] {'wide','narrow'}, dimensions={0} | all-to-all | bytes 393216 | tf_op jit(solution)/shard_map/all_to_all | solution.py:65
  364.5 0.1 copy.21
  364.6 0.8 copy.18
  365.4 0.0 copy-done.1
  (1 shorter events, 0.0 us)
Async XLA Ops:
  7.2 2.7 copy-start
  7.2 50.5 %all-gather.2.cloned.1.call-start = ((), (), s32[]{:S(2)}) async-start(), calls=%async_computation.3 | async-start | bytes 1769472 | tf_op jit(solution)/shard_map/all_gather | solution.py:50
  10.8 0.9 copy-start.2
  11.7 4.1 %copy-start.3 = (bf16[16,16384]{1,0:T(8,128)(2,1)S(1)}, bf16[16,16384]{1,0:T(8,128)(2,1)}, u32[]{:S(2)}) copy-start(bf16[16,16384]{1,0:T(8,128)(2,1)} %param.17) | copy-start | bytes 1572868
  11.7 4.1 %copy-start.4 = (bf16[6,16384]{1,0:T(8,128)(2,1)S(1)}, bf16[6,16384]{1,0:T(8,128)(2,1)}, u32[]{:S(2)}) copy-start(bf16[6,16384]{1,0:T(8,128)(2,1)} %param.11) | copy-start | bytes 589828
  11.7 4.1 %copy-start.5 = (s32[6]{0:T(128)S(1)}, s32[6]{0:T(128)}, u32[]{:S(2)}) copy-start(s32[6]{0:T(128)} %param.16) | copy-start | bytes 76
  32.9 253.6 %all-reduce.2.cloned.1.call-start = ((), (), s32[]{:S(2)}) async-start(), calls=%async_computation.4 | async-start | bytes 11010048 | tf_op jit(solution)/shard_map/psum | solution.py:58
  57.7 15.9 %copy-start.6 = (bf16[192,4096]{1,0:T(8,128)(2,1)S(1)}, bf16[192,4096]{1,0:T(8,128)(2,1)}, u32[]{:S(2)}) copy-start(bf16[192,4096]{1,0:T(8,128)(2,1)} %all-gather.2.cloned.1.call-done) | copy-start | bytes 4718596
  88.9 258.2 %reduce-scatter.2.cloned.1.call-start = ((), (), s32[]{:S(2)}) async-start(), calls=%async_computation.5 | async-start | bytes 3538944 | tf_op jit(solution)/shard_map/reduce_scatter | solution.py:63
  286.5 78.9 %copy-start.1 = (bf16[6,8,256,128]{3,2,1,0:T(8,128)(2,1)S(1)}, bf16[6,8,256,128]{3,2,1,0:T(8,128)(2,1)}, u32[]{:S(2)}) copy-start(bf16[6,8,256,128]{3,2,1,0:T(8,128)(2,1)} %param.13) | copy-start | bytes 9437188
Sparse Core Ops, SparseCore 0:
  33.0 24.6 all-gather.1
  89.0 197.3 all-reduce.1
  302.1 44.9 reduce-scatter.1
where the time goes:
time: 372 us
  waiting for transfers between devices  267 us (72%)
  matrix products  49.1 us (13%)
  blocking collectives  29.6 us (8%)
  between operations  13.8 us (4%)
  other arithmetic  7.21 us (2%)
  local copies, waits for them, and re-layouts  4.59 us (1%)
    psum x1, waiting for transfers between devices, per_device(): summed = lax.psum(partial_value, 'narrow')  198 us
    reduce_scatter x1, waiting for transfers between devices, per_device(): lax.psum_scatter(term, 'wide', scatter_dimension=1, tiled=True)  45.1 us
    all_gather x1, waiting for transfers between devices, per_device(): piece = lax.all_gather(columns, 'wide', axis=0, tiled=True)  24.8 us
    dot_general x1, matrix products, per_device(): jnp.dot(piece, up_weight, preferred_element_type=jnp.float32)  15.9 us
    dot_general x1, matrix products, per_device(): term = jnp.dot(hidden, down_weight, preferred_element_type=jnp.float32)  15.5 us
    all_to_all x1, blocking collectives, per_device(): lax.all_to_all(normed, 'narrow', split_axis=1, concat_axis=0, tiled=True)  15 us
    all_to_all x1, blocking collectives, per_device(): lax.all_to_all(slices, ('wide', 'narrow'), split_axis=0, concat_axis=1, t...  14.6 us
    dot_general x1, matrix products, per_device(): jnp.dot(piece, gate_weight, preferred_element_type=jnp.float32)  12.4 us
  transfers between devices with their start and end apart: 3, of which 3 were waited for; matrix products, arithmetic and copies ran while one was open for 0% of the time, Pallas kernels for 0%

commit v1 on v0

v1 whole, which is shorter than its diff:
```python
import functools
import math

import jax
import jax.numpy as jnp
from jax import lax
from jax.experimental import pallas as pl
from jax.experimental.pallas import tpu as pltpu
from jax.sharding import PartitionSpec as P

LAG = 2
VMEM_LIMIT = 66_000_000


def flip(index, bit):
    step = 2**bit
    return index + step * (1 - 2 * ((index // step) % 2))


def flips(index, bits):
    found = [index]
    for bit in bits:
        found = found + [flip(one, bit) for one in found]
    return found


def bit_orders(chips):
    count = chips.bit_length() - 1
    bits = list(range(count))
    half = count // 2
    return (bits, bits[half:] + bits[:half])


def meet(peers):
    barrier = pltpu.get_barrier_semaphore()
    for peer in peers:
        pl.semaphore_signal(barrier, inc=1, device_id=peer)
    pl.semaphore_wait(barrier, len(peers))


def gather_kernel(wide, narrow, mine_ref, out_ref, held, own_sem, z_send, z_recv, w_send, w_recv):
    w = lax.axis_index("wide")
    n = lax.axis_index("narrow")
    chips = wide // 2
    orders = bit_orders(chips)
    half = narrow // 2
    steps = wide.bit_length() - 1
    meet(
        [{"narrow": (n + i) % narrow} for i in range(1, narrow)]
        + [{"wide": flip(w, bit)} for bit in range(steps)]
    )

    own = pltpu.make_async_copy(mine_ref.at[n], held.at[w, n], own_sem)
    own.start()
    sends = []
    for i in range(1, narrow):
        to = (n + i) % narrow
        copy = pltpu.make_async_remote_copy(
            src_ref=mine_ref.at[to],
            dst_ref=held.at[w, n],
            send_sem=z_send.at[i],
            recv_sem=z_recv.at[n],
            device_id={"narrow": to},
        )
        copy.start()
        sends.append(copy)
    own.wait()
    for i in range(1, narrow):
        source = (n + i) % narrow
        pltpu.make_async_remote_copy(
            src_ref=mine_ref.at[source],
            dst_ref=held.at[w, source],
            send_sem=z_send.at[i],
            recv_sem=z_recv.at[source],
            device_id={"narrow": source},
        ).wait_recv()

    def block_copy(block, part, number, to):
        return pltpu.make_async_remote_copy(
            src_ref=held.at[block, pl.ds(part * half, half)],
            dst_ref=held.at[block, pl.ds(part * half, half)],
            send_sem=w_send.at[part, number],
            recv_sem=w_recv.at[part, block],
            device_id={"wide": to},
        )

    walks = [[bit + 1 for bit in order] + [0] for order in orders]
    number = 0
    for step in range(steps):
        for part in range(2):
            walk = walks[part]
            to = flip(w, walk[step])
            for k, block in enumerate(flips(w, walk[:step])):
                copy = block_copy(block, part, number + k, to)
                copy.start()
                sends.append(copy)
        for part in range(2):
            walk = walks[part]
            to = flip(w, walk[step])
            for k, block in enumerate(flips(to, walk[:step])):
                block_copy(block, part, number + k, to).wait_recv()
        number += 2**step
    for copy in sends:
        copy.wait_send()
    out_ref[...] = held[...]


def ffn_kernel(
    wide, narrow, chunks, ticks,
    piece_ref, gate_ref, up_ref, down_ref, out_ref,
    mine, arrived, hidden, total, down_held,
    sum_send, sum_recv, hid_send, hid_recv, down_sem,
):
    tick = pl.program_id(0)
    n = lax.axis_index("narrow")
    last = narrow - 1
    rows = mine.shape[3]
    width = mine.shape[4]
    features = total.shape[1]
    place = (n, last - n)
    onward = (jnp.minimum(n + 1, last), jnp.maximum(n - 1, 0))
    back = (jnp.maximum(n - 1, 0), jnp.minimum(n + 1, last))

    @pl.when(tick == 0)
    def _():
        barrier = pltpu.get_barrier_semaphore()

        @pl.when(n > 0)
        def _():
            pl.semaphore_signal(barrier, inc=1, device_id={"narrow": n - 1})

        @pl.when(n < last)
        def _():
            pl.semaphore_signal(barrier, inc=1, device_id={"narrow": n + 1})

        inner = (n > 0) & (n < last)

        @pl.when(inner)
        def _():
            pl.semaphore_wait(barrier, 2)

        @pl.when(jnp.logical_not(inner))
        def _():
            pl.semaphore_wait(barrier, 1)

    def down_copy(c):
        return pltpu.make_async_copy(
            down_ref.at[pl.ds(pl.multiple_of(c * width, width), width)],
            down_held.at[c],
            down_sem.at[c],
        )

    ahead = tick - LAG * last

    @pl.when((ahead >= 0) & (ahead < chunks))
    def _():
        down_copy(ahead).start()

    @pl.when(tick < chunks)
    def _():
        piece = piece_ref[...]
        gate = jnp.dot(piece, gate_ref[...], preferred_element_type=jnp.float32)
        up = jnp.dot(piece, up_ref[...], preferred_element_type=jnp.float32)
        for way in range(2):
            mine[tick, way, 0] = gate[way * rows : (way + 1) * rows].astype(jnp.bfloat16)
            mine[tick, way, 1] = up[way * rows : (way + 1) * rows].astype(jnp.bfloat16)

    def sum_copy(c, way):
        return pltpu.make_async_remote_copy(
            src_ref=mine.at[c, way],
            dst_ref=arrived.at[c, way],
            send_sem=sum_send.at[c, way],
            recv_sem=sum_recv.at[c, way],
            device_id={"narrow": onward[way]},
        )

    def hid_copy(c, way):
        return pltpu.make_async_remote_copy(
            src_ref=hidden.at[c, way],
            dst_ref=hidden.at[c, way],
            send_sem=hid_send.at[c, way],
            recv_sem=hid_recv.at[c, way],
            device_id={"narrow": back[way]},
        )

    for way in range(2):
        at = place[way]
        c = tick - LAG * at
        active = (c >= 0) & (c < chunks)

        @pl.when(active & (at > 0))
        def _():
            sum_copy(c, way).wait_recv()

        @pl.when(active & (at > 0) & (at < last))
        def _():
            mine[c, way] = (
                mine[c, way].astype(jnp.float32) + arrived[c, way].astype(jnp.float32)
            ).astype(jnp.bfloat16)

        @pl.when(active & (at < last))
        def _():
            sum_copy(c, way).start()

        @pl.when(active & (at == last))
        def _():
            gate = mine[c, way, 0].astype(jnp.float32) + arrived[c, way, 0].astype(jnp.float32)
            up = mine[c, way, 1].astype(jnp.float32) + arrived[c, way, 1].astype(jnp.float32)
            hidden[c, way] = (jax.nn.silu(gate) * up).astype(jnp.bfloat16)
            hid_copy(c, way).start()

        b = tick - LAG * last - LAG * (last - at)
        relayed = (b >= 0) & (b < chunks) & (at < last)

        @pl.when(relayed)
        def _():
            hid_copy(b, way).wait_recv()

        @pl.when(relayed & (at > 0))
        def _():
            hid_copy(b, way).start()

    ready = tick - LAG * 2 * last

    @pl.when((ready >= 0) & (ready < chunks))
    def _():
        down_copy(ready).wait()
        left = hidden[ready].reshape(2 * rows, width)
        tile = 512

        def add(j, carry):
            columns = pl.ds(pl.multiple_of(j * tile, tile), tile)
            term = jnp.dot(left, down_held[ready, :, columns], preferred_element_type=jnp.float32)

            @pl.when(ready == 0)
            def _():
                total[:, columns] = term

            @pl.when(ready > 0)
            def _():
                total[:, columns] += term

            return carry

        lax.fori_loop(0, features // tile, add, 0)

    @pl.when(tick == ticks - 1)
    def _():
        for way in range(2):
            at = place[way]

            def ended(c, carry):
                @pl.when(at < last)
                def _():
                    sum_copy(c, way).wait_send()

                @pl.when(at > 0)
                def _():
                    hid_copy(c, way).wait_send()

                return carry

            lax.fori_loop(0, chunks, ended, 0)
        share = features // wide
        for k in range(wide):
            out_ref[k] = total[:, k * share : (k + 1) * share].astype(jnp.bfloat16)


def scatter_kernel(
    wide, narrow, term_ref, out_ref,
    near, held, far, summed, parts, landed,
    c_send, c_recv, w_send, w_recv, a_send, a_recv,
):
    w = lax.axis_index("wide")
    n = lax.axis_index("narrow")
    me = w * narrow + n
    devices = wide * narrow
    chips = wide // 2
    core = w % 2
    chip = w // 2
    rows = term_ref.shape[1]
    half = rows // 2
    own_rows = rows // devices
    share = term_ref.shape[2]
    orders = bit_orders(chips)
    steps = chips.bit_length() - 1
    barrier = pltpu.get_barrier_semaphore()

    def greet(i, carry):
        peer = (me + i) % devices
        pl.semaphore_signal(
            barrier, inc=1, device_id={"wide": peer // narrow, "narrow": peer % narrow}
        )
        return carry

    lax.fori_loop(1, devices, greet, 0)
    pl.semaphore_wait(barrier, devices - 1)

    def core_copy(k):
        return pltpu.make_async_remote_copy(
            src_ref=term_ref.at[2 * k + 1 - core],
            dst_ref=near.at[k],
            send_sem=c_send.at[k],
            recv_sem=c_recv.at[k],
            device_id={"wide": flip(w, 0)},
        )

    for k in range(chips):
        core_copy(k).start()
    for k in range(chips):
        core_copy(k).wait_recv()
        held[k] = (
            term_ref[2 * k + core].astype(jnp.float32) + near[k].astype(jnp.float32)
        ).astype(jnp.bfloat16)

    def chip_copy(block, part, step, number, to):
        span = pl.ds(part * half, half)
        return pltpu.make_async_remote_copy(
            src_ref=held.at[block, span],
            dst_ref=far.at[step, block, span],
            send_sem=w_send.at[part, number],
            recv_sem=w_recv.at[part, number],
            device_id={"wide": 2 * to + core},
        )

    sends = []
    number = 0
    for step in range(steps):
        for part in range(2):
            order = orders[part]
            to = flip(chip, order[step])
            for k, block in enumerate(flips(to, order[step + 1 :])):
                copy = chip_copy(block, part, step, number + k, to)
                copy.start()
                sends.append(copy)
        for part in range(2):
            order = orders[part]
            to = flip(chip, order[step])
            span = pl.ds(part * half, half)
            for k, block in enumerate(flips(chip, order[step + 1 :])):
                chip_copy(block, part, step, number + k, to).wait_recv()
                value = held[block, span].astype(jnp.float32) + far[step, block, span].astype(
                    jnp.float32
                )
                if step < steps - 1:
                    held[block, span] = value.astype(jnp.bfloat16)
                else:
                    summed[span] = value
        number += 2 ** (steps - 1 - step)

    for i in range(devices):
        parts[i] = summed[i * own_rows : (i + 1) * own_rows].astype(jnp.bfloat16)

    def part_copy(to, source):
        return pltpu.make_async_remote_copy(
            src_ref=parts.at[to],
            dst_ref=landed.at[source],
            send_sem=a_send.at[to],
            recv_sem=a_recv.at[source],
            device_id={"wide": to // narrow, "narrow": to % narrow},
        )

    def send(i, carry):
        part_copy((me + i) % devices, me).start()
        return carry

    lax.fori_loop(1, devices, send, 0)
    landed[me] = parts[me]
    for k in range(chips):
        core_copy(k).wait_send()
    for copy in sends:
        copy.wait_send()

    def finish(i, carry):
        other = (me + i) % devices
        part_copy(other, other).wait_recv()
        part_copy(other, other).wait_send()
        return carry

    lax.fori_loop(1, devices, finish, 0)
    for i in range(wide):
        for j in range(narrow):
            start = (j * wide + i) * share
            out_ref[:, start : start + share] = landed[i * narrow + j]


def per_device(
    wide,
    narrow,
    residual,
    queries,
    keys,
    values,
    cache_lengths,
    track_numbers,
    track_table,
    norm_gain,
    gate_weight,
    up_weight,
    down_weight,
):
    batch_rows, model = residual.shape
    key_heads = keys.shape[1]
    cache_size = keys.shape[2]
    head_size = keys.shape[3]
    grouped = queries.reshape(batch_rows, key_heads, -1, head_size)
    scores = jnp.einsum(
        "bkgd,bkld->bkgl", grouped, keys, preferred_element_type=jnp.float32
    ) / math.sqrt(head_size)
    visible = jnp.arange(cache_size, dtype=jnp.int32)[None, :] < cache_lengths[:, None]
    scores = jnp.where(visible[:, None, None, :], scores, -jnp.inf)
    highest = jnp.max(scores, axis=-1, keepdims=True)
    weights = jnp.exp(scores - highest)
    probs = (weights / jnp.sum(weights, axis=-1, keepdims=True)).astype(jnp.bfloat16)
    context = jnp.einsum(
        "bkgl,bkld->bkgd", probs, values, preferred_element_type=jnp.float32
    ).reshape(batch_rows, -1)
    one_hot = (
        track_numbers[:, None] == jnp.arange(track_table.shape[0], dtype=jnp.int32)[None, :]
    ).astype(jnp.bfloat16)
    stream = (
        residual.astype(jnp.float32)
        + context
        + jnp.dot(one_hot, track_table, preferred_element_type=jnp.float32)
    )
    attended = stream.astype(jnp.bfloat16)
    scale = lax.rsqrt(jnp.mean(stream * stream, axis=-1, keepdims=True) + 1e-05)
    normed = (stream * scale * norm_gain.astype(jnp.float32)).astype(jnp.bfloat16)

    depth = model // narrow
    devices = wide * narrow
    rows = batch_rows * devices
    vmem = pl.BlockSpec(memory_space=pltpu.VMEM)
    dma = pltpu.SemaphoreType.DMA
    bf16 = jnp.bfloat16
    split = normed.reshape(batch_rows, narrow, depth).transpose(1, 0, 2)
    gathered = pl.pallas_call(
        functools.partial(gather_kernel, wide, narrow),
        out_shape=jax.ShapeDtypeStruct((wide, narrow, batch_rows, depth), bf16),
        in_specs=[vmem],
        out_specs=vmem,
        scratch_shapes=[
            pltpu.VMEM((wide, narrow, batch_rows, depth), bf16),
            dma(()),
            dma((narrow,)),
            dma((narrow,)),
            dma((2, wide)),
            dma((2, wide)),
        ],
        compiler_params=pltpu.CompilerParams(
            collective_id=0, has_side_effects=True, vmem_limit_bytes=VMEM_LIMIT
        ),
        name="gather",
    )(split)
    piece = gathered.reshape(rows, depth)

    columns = gate_weight.shape[1]
    width = 256 if columns % 256 == 0 else 128
    chunks = columns // width
    ticks = chunks + LAG * 2 * (narrow - 1)
    share = depth // wide
    term = pl.pallas_call(
        functools.partial(ffn_kernel, wide, narrow, chunks, ticks),
        grid=(ticks,),
        out_shape=jax.ShapeDtypeStruct((wide, rows, share), bf16),
        in_specs=[
            pl.BlockSpec((rows, depth), lambda i: (0, 0)),
            pl.BlockSpec((depth, width), lambda i: (0, jnp.minimum(i, chunks - 1))),
            pl.BlockSpec((depth, width), lambda i: (0, jnp.minimum(i, chunks - 1))),
            pl.BlockSpec(memory_space=pl.ANY),
        ],
        out_specs=pl.BlockSpec((wide, rows, share), lambda i: (0, 0, 0)),
        scratch_shapes=[
            pltpu.VMEM((chunks, 2, 2, rows // 2, width), bf16),
            pltpu.VMEM((chunks, 2, 2, rows // 2, width), bf16),
            pltpu.VMEM((chunks, 2, rows // 2, width), bf16),
            pltpu.VMEM((rows, depth), jnp.float32),
            pltpu.VMEM((chunks, width, depth), bf16),
            dma((chunks, 2)),
            dma((chunks, 2)),
            dma((chunks, 2)),
            dma((chunks, 2)),
            dma((chunks,)),
        ],
        compiler_params=pltpu.CompilerParams(
            collective_id=1, has_side_effects=True, vmem_limit_bytes=VMEM_LIMIT
        ),
        name="ffn",
    )(piece, gate_weight, up_weight, down_weight)

    chips = wide // 2
    steps = chips.bit_length() - 1
    ffn_out = pl.pallas_call(
        functools.partial(scatter_kernel, wide, narrow),
        out_shape=jax.ShapeDtypeStruct((batch_rows, model), bf16),
        in_specs=[vmem],
        out_specs=vmem,
        scratch_shapes=[
            pltpu.VMEM((chips, rows, share), bf16),
            pltpu.VMEM((chips, rows, share), bf16),
            pltpu.VMEM((steps, chips, rows, share), bf16),
            pltpu.VMEM((rows, share), jnp.float32),
            pltpu.VMEM((devices, batch_rows, share), bf16),
            pltpu.VMEM((devices, batch_rows, share), bf16),
            dma((chips,)),
            dma((chips,)),
            dma((2, chips)),
            dma((2, chips)),
            dma((devices,)),
            dma((devices,)),
        ],
        compiler_params=pltpu.CompilerParams(
            collective_id=2, has_side_effects=True, vmem_limit_bytes=VMEM_LIMIT
        ),
        name="scatter",
    )(term)
    return (attended, ffn_out)


def solution(mesh):
    in_specs = (
        P(("wide", "narrow"), None),
        P(("wide", "narrow"), None),
        P(("wide", "narrow"), None, None, None),
        P(("wide", "narrow"), None, None, None),
        P(("wide", "narrow")),
        P(("wide", "narrow")),
        P(),
        P(),
        P("narrow", "wide"),
        P("narrow", "wide"),
        P("wide", "narrow"),
    )
    out_specs = (P(("wide", "narrow"), None), P(("wide", "narrow"), None))
    return jax.shard_map(
        functools.partial(per_device, mesh.shape["wide"], mesh.shape["narrow"]),
        mesh=mesh,
        in_specs=in_specs,
        out_specs=out_specs,
        check_vma=False,
    )
```

time: 372 us -> 144 us (0.39)
  waiting for transfers between devices: 267 us -> 0 us
  Pallas kernels: 0 us -> 127 us
  matrix products: 49.1 us -> 6.64 us
  blocking collectives: 29.6 us -> 0 us
  between operations: 13.8 us -> 0.7 us
  other arithmetic: 7.21 us -> 2.68 us
    psum x1 -> x0, waiting for transfers between devices: 198 us -> none  [per_device(): summed = lax.psum(partial_value, 'narrow')]
    pallas_call x0 -> x3, Pallas kernels: none -> 127 us  [the longest x1 74.7 us: per_device(): pl.pallas_call(functools.partial(ffn_kernel, wide, narrow, chunks, ticks)...]
    reduce_scatter x1 -> x0, waiting for transfers between devices: 45.1 us -> none  [per_device(): lax.psum_scatter(term, 'wide', scatter_dimension=1, tiled=True)]
    dot_general x3 -> x0, matrix products: 43.8 us -> none  [the longest x1 15.9 us: per_device(): jnp.dot(piece, up_weight, preferred_element_type=jnp.float32)]
    all_to_all x2 -> x0, blocking collectives: 29.6 us -> none  [the longest x1 15 us: per_device(): lax.all_to_all(normed, 'narrow', split_axis=1, concat_axis=0, tiled=True)]
    all_gather x1 -> x0, waiting for transfers between devices: 24.8 us -> none  [per_device(): piece = lax.all_gather(columns, 'wide', axis=0, tiled=True)]
  transfers between devices with their start and end apart: 3 -> 0, of which waited for: 3 -> 0; matrix products, arithmetic and copies ran while one was open for 0% -> 0% of each run, Pallas kernels for 0% -> 0%
where the time goes in v1:
time: 144 us
  Pallas kernels  127 us (88%)
  matrix products  6.64 us (5%)
  local copies, waits for them, and re-layouts  6.36 us (4%)
  other arithmetic  2.68 us (2%)
    pallas_call x1, Pallas kernels, per_device(): pl.pallas_call(functools.partial(ffn_kernel, wide, narrow, chunks, ticks)...  74.7 us
    pallas_call x1, Pallas kernels, per_device(): pl.pallas_call(functools.partial(gather_kernel, wide, narrow), out_shape=...  27.2 us
    pallas_call x1, Pallas kernels, per_device(): pl.pallas_call(functools.partial(scatter_kernel, wide, narrow), out_shape...  25.2 us
    reshape x1, local copies, waits for them, and re-layouts, per_device(): piece = gathered.reshape(rows, depth)  3.67 us
    dot_general x1, matrix products, per_device(): jnp.einsum('bkgl,bkld->bkgd', probs, values, preferred_element_type=jnp.f...  3.3 us

profile of v1, /device:TPU:0, one launch (start us, length us, event | category | flops | bytes accessed | tf_op | source)
XLA Modules:
  0.0 143.5 jit_solution(195045684839605744)
XLA Ops:
  0.6 0.0 copy-start
  0.6 0.8 iota_compare_fusion
  1.4 0.8 convert_element_type.19
  2.2 1.0 copy.13
  3.2 2.8 %fusion.3 = f32[6,8,16,256]{3,2,1,0:T(8,128)S(1)} fusion(bf16[6,8,16,128]{3,2,1,0:T(8,128)(2,1)S(1)} %bitcast.19, bf16[6,8,256,128]{3,2,1,0:T(8,128)(2,1)} %param.13, pred[6,256]{1,0:T(8,128)(4,1)S(1)} %iota_compare_fusion), kind=kOutput, calls=%fused_computation.5 | convolution fusion | flops 50724864 | bytes 4130304 | tf_op jit(solution)/shard_map/bkgd,bkld->bkgl/dot_general | solution.py:407
  6.0 0.0 copy-start.2
  6.0 0.0 copy-start.3
  6.0 0.3 fusion.8
  6.3 3.3 %fusion.4 = f32[6,8,16,128]{3,2,1,0:T(8,128)S(1)} fusion(bf16[6,8,256,128]{3,2,1,0:T(8,128)(2,1)} %param.14, f32[6,8,16]{2,1,0:T(8,128)S(1)} %fusion.8, f32[6,8,16,256]{3,2,1,0:T(8,128)S(1)} %fusion.3), kind=kOutput, calls=%fused_computation.10 | convolution fusion | flops 50922496 | bytes 4328448 | tf_op jit(solution)/shard_map/bkgl,bkld->bkgd/dot_general | solution.py:415
  9.6 0.0 copy-done
  9.6 0.0 copy-done.2
  9.6 0.0 copy-done.3
  9.6 0.5 multiply_reduce_fusion
  10.2 0.8 multiply_convert_fusion
  11.0 27.2 %gather.1 = bf16[8,4,6,4096]{3,2,1,0:T(8,128)(2,1)} custom-call(bf16[4,6,4096]{2,1,0:T(8,128)(2,1)} %bitcast.18), custom_call_target="tpu_custom_call" | custom-call | tf_op jit(solution)/shard_map/gather/pallas_call | solution.py:437
  38.3 3.7 %reshape.48.piece_ref = bf16[192,4096]{1,0:T(8,128)(2,1)} reshape(bf16[8,4,6,4096]{3,2,1,0:T(8,128)(2,1)} %gather.1) | data formatting | bytes 3145728 | tf_op jit(solution)/shard_map/reshape | solution.py:455
  41.9 0.0 copy-start.1
  41.9 74.7 %ffn.1.term_ref = bf16[8,192,512]{2,1,0:T(8,128)(2,1)} custom-call(bf16[192,4096]{1,0:T(8,128)(2,1)} %reshape.48.piece_ref, bf16[4096,3584]{1,0:T(8,128)(2,1)} %gate_ref.1, bf16[4096,3584]{1,0:T(8,128)(2,1)} %up_ref.1, bf16[3584,4096]{1,0:T(8,128)(2,1)} %down_ref.1), custom_call_target="tpu_custom_call" | custom-call | tf_op jit(solution)/shard_map/ffn/pallas_call | solution.py:462
  116.6 25.2 %scatter.1 = bf16[6,16384]{1,0:T(8,128)(2,1)} custom-call(bf16[8,192,512]{2,1,0:T(8,128)(2,1)} %ffn.1.term_ref), custom_call_target="tpu_custom_call" | custom-call | tf_op jit(solution)/shard_map/scatter/pallas_call | solution.py:493
  141.8 1.7 %copy.17 = bf16[6,16384]{1,0:T(8,128)(2,1)} copy(bf16[6,16384]{1,0:T(8,128)(2,1)} %scatter.1) | data formatting | bytes 393216
  143.5 0.0 copy-done.1
  (1 shorter events, 0.0 us)
Async XLA Ops:
  0.6 9.0 %copy-start = (bf16[16,16384]{1,0:T(8,128)(2,1)S(1)}, bf16[16,16384]{1,0:T(8,128)(2,1)}, u32[]{:S(2)}) copy-start(bf16[16,16384]{1,0:T(8,128)(2,1)} %param.17) | copy-start | bytes 1572868
  6.0 3.6 %copy-start.2 = (bf16[6,16384]{1,0:T(8,128)(2,1)S(1)}, bf16[6,16384]{1,0:T(8,128)(2,1)}, u32[]{:S(2)}) copy-start(bf16[6,16384]{1,0:T(8,128)(2,1)} %param.11) | copy-start | bytes 589828
  6.0 3.6 %copy-start.3 = (s32[6]{0:T(128)S(1)}, s32[6]{0:T(128)}, u32[]{:S(2)}) copy-start(s32[6]{0:T(128)} %param.16) | copy-start | bytes 76
  41.9 101.6 %copy-start.1 = (bf16[16,16384]{1,0:T(8,128)(2,1)S(1)}, bf16[16,16384]{1,0:T(8,128)(2,1)}, u32[]{:S(2)}) copy-start(bf16[16,16384]{1,0:T(8,128)(2,1)} %param.17) | copy-start | bytes 1572868

commit v2 on v1

--- a/solution.py
+++ b/solution.py
@@ -9,6 +9,7 @@
 from jax.sharding import PartitionSpec as P
 
 LAG = 2
+BACK = 1
 VMEM_LIMIT = 66_000_000
 
 
@@ -107,8 +108,8 @@
 
 def ffn_kernel(
     wide, narrow, chunks, ticks,
-    piece_ref, gate_ref, up_ref, down_ref, out_ref,
-    mine, arrived, hidden, total, down_held,
+    piece_ref, gate_ref, up_ref, down_ref, keep_ref, give_ref,
+    mine, sent, arrived, hidden, total, down_held,
     sum_send, sum_recv, hid_send, hid_recv, down_sem,
 ):
     tick = pl.program_id(0)
@@ -116,7 +117,7 @@
     last = narrow - 1
     rows = mine.shape[3]
     width = mine.shape[4]
-    features = total.shape[1]
+    slots = mine.shape[0]
     place = (n, last - n)
     onward = (jnp.minimum(n + 1, last), jnp.maximum(n - 1, 0))
     back = (jnp.maximum(n - 1, 0), jnp.minimum(n + 1, last))
@@ -162,12 +163,12 @@
         gate = jnp.dot(piece, gate_ref[...], preferred_element_type=jnp.float32)
         up = jnp.dot(piece, up_ref[...], preferred_element_type=jnp.float32)
         for way in range(2):
-            mine[tick, way, 0] = gate[way * rows : (way + 1) * rows].astype(jnp.bfloat16)
-            mine[tick, way, 1] = up[way * rows : (way + 1) * rows].astype(jnp.bfloat16)
+            mine[tick % slots, way, 0] = gate[way * rows : (way + 1) * rows]
+            mine[tick % slots, way, 1] = up[way * rows : (way + 1) * rows]
 
     def sum_copy(c, way):
         return pltpu.make_async_remote_copy(
-            src_ref=mine.at[c, way],
+            src_ref=sent.at[c, way],
             dst_ref=arrived.at[c, way],
             send_sem=sum_send.at[c, way],
             recv_sem=sum_recv.at[c, way],
@@ -192,11 +193,17 @@
         def _():
             sum_copy(c, way).wait_recv()
 
+        slot = (c + slots) % slots
+
+        @pl.when(active & (at == 0))
+        def _():
+            sent[c, way] = mine[slot, way].astype(jnp.bfloat16)
+
         @pl.when(active & (at > 0) & (at < last))
         def _():
-            mine[c, way] = (
-                mine[c, way].astype(jnp.float32) + arrived[c, way].astype(jnp.float32)
-            ).astype(jnp.bfloat16)
+            sent[c, way] = (mine[slot, way] + arrived[c, way].astype(jnp.float32)).astype(
+                jnp.bfloat16
+            )
 
         @pl.when(active & (at < last))
         def _():
@@ -204,12 +211,12 @@
 
         @pl.when(active & (at == last))
         def _():
-            gate = mine[c, way, 0].astype(jnp.float32) + arrived[c, way, 0].astype(jnp.float32)
-            up = mine[c, way, 1].astype(jnp.float32) + arrived[c, way, 1].astype(jnp.float32)
+            gate = mine[slot, way, 0] + arrived[c, way, 0].astype(jnp.float32)
+            up = mine[slot, way, 1] + arrived[c, way, 1].astype(jnp.float32)
             hidden[c, way] = (jax.nn.silu(gate) * up).astype(jnp.bfloat16)
             hid_copy(c, way).start()
 
-        b = tick - LAG * last - LAG * (last - at)
+        b = tick - LAG * last - BACK * (last - at)
         relayed = (b >= 0) & (b < chunks) & (at < last)
 
         @pl.when(relayed)
@@ -220,29 +227,29 @@
         def _():
             hid_copy(b, way).start()
 
-    ready = tick - LAG * 2 * last
+    ready = tick - (LAG + BACK) * last
 
     @pl.when((ready >= 0) & (ready < chunks))
     def _():
         down_copy(ready).wait()
         left = hidden[ready].reshape(2 * rows, width)
-        tile = 512
+        share = total.shape[2]
 
         def add(j, carry):
-            columns = pl.ds(pl.multiple_of(j * tile, tile), tile)
+            columns = pl.ds(pl.multiple_of(j * share, share), share)
             term = jnp.dot(left, down_held[ready, :, columns], preferred_element_type=jnp.float32)
 
             @pl.when(ready == 0)
             def _():
-                total[:, columns] = term
+                total[j] = term
 
             @pl.when(ready > 0)
             def _():
-                total[:, columns] += term
+                total[j] += term
 
             return carry
 
-        lax.fori_loop(0, features // tile, add, 0)
+        lax.fori_loop(0, wide, add, 0)
 
     @pl.when(tick == ticks - 1)
     def _():
@@ -261,14 +268,15 @@
                 return carry
 
             lax.fori_loop(0, chunks, ended, 0)
-        share = features // wide
-        for k in range(wide):
-            out_ref[k] = total[:, k * share : (k + 1) * share].astype(jnp.bfloat16)
+        core = lax.axis_index("wide") % 2
+        for k in range(wide // 2):
+            keep_ref[k] = total[2 * k + core]
+            give_ref[k] = total[2 * k + 1 - core].astype(jnp.bfloat16)
 
 
 def scatter_kernel(
-    wide, narrow, term_ref, out_ref,
-    near, held, far, summed, parts, landed,
+    wide, narrow, keep_ref, give_ref, out_ref,
+    near, held, wire, far, summed, parts, landed,
     c_send, c_recv, w_send, w_recv, a_send, a_recv,
 ):
     w = lax.axis_index("wide")
@@ -278,10 +286,10 @@
     chips = wide // 2
     core = w % 2
     chip = w // 2
-    rows = term_ref.shape[1]
+    rows = keep_ref.shape[1]
     half = rows // 2
     own_rows = rows // devices
-    share = term_ref.shape[2]
+    share = keep_ref.shape[2]
     orders = bit_orders(chips)
     steps = chips.bit_length() - 1
     barrier = pltpu.get_barrier_semaphore()
@@ -298,7 +306,7 @@
 
     def core_copy(k):
         return pltpu.make_async_remote_copy(
-            src_ref=term_ref.at[2 * k + 1 - core],
+            src_ref=give_ref.at[k],
             dst_ref=near.at[k],
             send_sem=c_send.at[k],
             recv_sem=c_recv.at[k],
@@ -309,14 +317,12 @@
         core_copy(k).start()
     for k in range(chips):
         core_copy(k).wait_recv()
-        held[k] = (
-            term_ref[2 * k + core].astype(jnp.float32) + near[k].astype(jnp.float32)
-        ).astype(jnp.bfloat16)
+        held[k] = keep_ref[k] + near[k].astype(jnp.float32)
 
     def chip_copy(block, part, step, number, to):
         span = pl.ds(part * half, half)
         return pltpu.make_async_remote_copy(
-            src_ref=held.at[block, span],
+            src_ref=wire.at[block, span],
             dst_ref=far.at[step, block, span],
             send_sem=w_send.at[part, number],
             recv_sem=w_recv.at[part, number],
@@ -330,6 +336,8 @@
             order = orders[part]
             to = flip(chip, order[step])
             for k, block in enumerate(flips(to, order[step + 1 :])):
+                span = pl.ds(part * half, half)
+                wire[block, span] = held[block, span].astype(jnp.bfloat16)
                 copy = chip_copy(block, part, step, number + k, to)
                 copy.start()
                 sends.append(copy)
@@ -339,11 +347,11 @@
             span = pl.ds(part * half, half)
             for k, block in enumerate(flips(chip, order[step + 1 :])):
                 chip_copy(block, part, step, number + k, to).wait_recv()
-                value = held[block, span].astype(jnp.float32) + far[step, block, span].astype(
+                value = held[block, span] + far[step, block, span].astype(
                     jnp.float32
                 )
                 if step < steps - 1:
-                    held[block, span] = value.astype(jnp.bfloat16)
+                    held[block, span] = value
                 else:
                     summed[span] = value
         number += 2 ** (steps - 1 - step)
@@ -433,14 +441,19 @@
     vmem = pl.BlockSpec(memory_space=pltpu.VMEM)
     dma = pltpu.SemaphoreType.DMA
     bf16 = jnp.bfloat16
-    split = normed.reshape(batch_rows, narrow, depth).transpose(1, 0, 2)
+    lines = batch_rows * depth // 128
+    split = (
+        normed.reshape(batch_rows, narrow, depth // 128, 128)
+        .transpose(1, 0, 2, 3)
+        .reshape(narrow, lines, 128)
+    )
     gathered = pl.pallas_call(
         functools.partial(gather_kernel, wide, narrow),
-        out_shape=jax.ShapeDtypeStruct((wide, narrow, batch_rows, depth), bf16),
+        out_shape=jax.ShapeDtypeStruct((wide, narrow, lines, 128), bf16),
         in_specs=[vmem],
         out_specs=vmem,
         scratch_shapes=[
-            pltpu.VMEM((wide, narrow, batch_rows, depth), bf16),
+            pltpu.VMEM((wide, narrow, lines, 128), bf16),
             dma(()),
             dma((narrow,)),
             dma((narrow,)),
@@ -457,24 +470,30 @@
     columns = gate_weight.shape[1]
     width = 256 if columns % 256 == 0 else 128
     chunks = columns // width
-    ticks = chunks + LAG * 2 * (narrow - 1)
+    slots = LAG * (narrow - 1) + 1
+    ticks = chunks + (LAG + BACK) * (narrow - 1)
+    chips = wide // 2
     share = depth // wide
-    term = pl.pallas_call(
+    keep, give = pl.pallas_call(
         functools.partial(ffn_kernel, wide, narrow, chunks, ticks),
         grid=(ticks,),
-        out_shape=jax.ShapeDtypeStruct((wide, rows, share), bf16),
+        out_shape=(
+            jax.ShapeDtypeStruct((chips, rows, share), jnp.float32),
+            jax.ShapeDtypeStruct((chips, rows, share), bf16),
+        ),
         in_specs=[
-            pl.BlockSpec((rows, depth), lambda i: (0, 0)),
+            pl.BlockSpec((rows, depth), lambda i: (0, 0), pipeline_mode=pl.Buffered(1)),
             pl.BlockSpec((depth, width), lambda i: (0, jnp.minimum(i, chunks - 1))),
             pl.BlockSpec((depth, width), lambda i: (0, jnp.minimum(i, chunks - 1))),
             pl.BlockSpec(memory_space=pl.ANY),
         ],
-        out_specs=pl.BlockSpec((wide, rows, share), lambda i: (0, 0, 0)),
+        out_specs=(pl.BlockSpec((chips, rows, share), lambda i: (0, 0, 0)),) * 2,
         scratch_shapes=[
+            pltpu.VMEM((slots, 2, 2, rows // 2, width), jnp.float32),
             pltpu.VMEM((chunks, 2, 2, rows // 2, width), bf16),
             pltpu.VMEM((chunks, 2, 2, rows // 2, width), bf16),
             pltpu.VMEM((chunks, 2, rows // 2, width), bf16),
-            pltpu.VMEM((rows, depth), jnp.float32),
+            pltpu.VMEM((wide, rows, share), jnp.float32),
             pltpu.VMEM((chunks, width, depth), bf16),
             dma((chunks, 2)),
             dma((chunks, 2)),
@@ -488,15 +507,15 @@
         name="ffn",
     )(piece, gate_weight, up_weight, down_weight)
 
-    chips = wide // 2
     steps = chips.bit_length() - 1
     ffn_out = pl.pallas_call(
         functools.partial(scatter_kernel, wide, narrow),
         out_shape=jax.ShapeDtypeStruct((batch_rows, model), bf16),
-        in_specs=[vmem],
+        in_specs=[vmem, vmem],
         out_specs=vmem,
         scratch_shapes=[
             pltpu.VMEM((chips, rows, share), bf16),
+            pltpu.VMEM((chips, rows, share), jnp.float32),
             pltpu.VMEM((chips, rows, share), bf16),
             pltpu.VMEM((steps, chips, rows, share), bf16),
             pltpu.VMEM((rows, share), jnp.float32),
@@ -513,7 +532,7 @@
             collective_id=2, has_side_effects=True, vmem_limit_bytes=VMEM_LIMIT
         ),
         name="scatter",
-    )(term)
+    )(keep, give)
     return (attended, ffn_out)
 
 

time: 144 us -> 146 us (1.014)
    pallas_call x1, Pallas kernels: 74.7 us -> 78.3 us  [per_device(): pl.pallas_call(functools.partial(ffn_kernel, wide, narrow, chunks, ticks)...]
    pallas_call x1, Pallas kernels: 27.2 us -> 24.5 us  [per_device(): pl.pallas_call(functools.partial(gather_kernel, wide, narrow), out_shape=...]
where the time goes in v2:
time: 146 us
  Pallas kernels  128 us (88%)
  local copies, waits for them, and re-layouts  7.1 us (5%)
  matrix products  6.64 us (5%)
  other arithmetic  2.59 us (2%)
    pallas_call x1, Pallas kernels, per_device(): pl.pallas_call(functools.partial(ffn_kernel, wide, narrow, chunks, ticks)...  78.3 us
    pallas_call x1, Pallas kernels, per_device(): pl.pallas_call(functools.partial(scatter_kernel, wide, narrow), out_shape...  25.7 us
    pallas_call x1, Pallas kernels, per_device(): pl.pallas_call(functools.partial(gather_kernel, wide, narrow), out_shape=...  24.5 us
    reshape x1, local copies, waits for them, and re-layouts, per_device(): piece = gathered.reshape(rows, depth)  3.71 us
    dot_general x1, matrix products, per_device(): jnp.einsum('bkgl,bkld->bkgd', probs, values, preferred_element_type=jnp.f...  3.3 us

profile of v2, /device:TPU:0, one launch (start us, length us, event | category | flops | bytes accessed | tf_op | source)
XLA Modules:
  0.0 145.5 jit_solution(12052875770556232374)
XLA Ops:
  0.6 0.0 copy-start
  0.6 0.8 iota_compare_fusion
  1.4 0.8 convert_element_type.19
  2.2 1.0 copy.14
  3.2 2.8 %fusion.3 = f32[6,8,16,256]{3,2,1,0:T(8,128)S(1)} fusion(bf16[6,8,16,128]{3,2,1,0:T(8,128)(2,1)S(1)} %bitcast.26, bf16[6,8,256,128]{3,2,1,0:T(8,128)(2,1)} %param.13, pred[6,256]{1,0:T(8,128)(4,1)S(1)} %iota_compare_fusion), kind=kOutput, calls=%fused_computation.5 | convolution fusion | flops 50724864 | bytes 4130304 | tf_op jit(solution)/shard_map/bkgd,bkld->bkgl/dot_general | solution.py:415
  6.0 0.0 copy-start.2
  6.0 0.0 copy-start.3
  6.0 0.3 fusion.9
  6.3 3.3 %fusion.4 = f32[6,8,16,128]{3,2,1,0:T(8,128)S(1)} fusion(bf16[6,8,256,128]{3,2,1,0:T(8,128)(2,1)} %param.14, f32[6,8,16]{2,1,0:T(8,128)S(1)} %fusion.9, f32[6,8,16,256]{3,2,1,0:T(8,128)S(1)} %fusion.3), kind=kOutput, calls=%fused_computation.10 | convolution fusion | flops 50922496 | bytes 4328448 | tf_op jit(solution)/shard_map/bkgl,bkld->bkgd/dot_general | solution.py:423
  9.6 0.0 copy-done
  9.6 0.0 copy-done.2
  9.6 0.0 copy-done.3
  9.6 0.5 multiply_reduce_fusion
  10.2 0.8 fusion.6
  10.9 0.7 copy.13
  11.6 24.5 %gather.1 = bf16[8,4,192,128]{3,2,1,0:T(8,128)(2,1)} custom-call(bf16[4,192,128]{2,1,0:T(8,128)(2,1)} %bitcast.27), custom_call_target="tpu_custom_call" | custom-call | tf_op jit(solution)/shard_map/gather/pallas_call | solution.py:450
  36.1 3.7 %reshape.52.piece_ref = bf16[192,4096]{1,0:T(8,128)(2,1)} reshape(bf16[8,4,192,128]{3,2,1,0:T(8,128)(2,1)} %gather.1) | data formatting | bytes 3145728 | tf_op jit(solution)/shard_map/reshape | solution.py:468
  39.8 0.0 copy-start.1
  39.8 78.3 %ffn.1 = (f32[4,192,512]{2,1,0:T(8,128)}, bf16[4,192,512]{2,1,0:T(8,128)(2,1)}) custom-call(bf16[192,4096]{1,0:T(8,128)(2,1)} %reshape.52.piece_ref, bf16[4096,3584]{1,0:T(8,128)(2,1)} %gate_ref.1, bf16[4096,3584]{1,0:T(8,128)(2,1)} %up_ref.1, bf16[3584,4096]{1,0:T(8,128)(2,1)} %down_ref.1), custom_call_target="tpu_custom_call" | custom-call | tf_op jit(solution)/shard_map/ffn/pallas_call | solution.py:477
  118.2 25.7 %scatter.1 = bf16[6,16384]{1,0:T(8,128)(2,1)} custom-call(f32[4,192,512]{2,1,0:T(8,128)} %get-tuple-element.4.keep_ref, bf16[4,192,512]{2,1,0:T(8,128)(2,1)} %get-tuple-element.5.give_ref), custom_call_target="tpu_custom_call" | custom-call | tf_op jit(solution)/shard_map/scatter/pallas_call | solution.py:511
  143.8 1.7 %copy.20 = bf16[6,16384]{1,0:T(8,128)(2,1)} copy(bf16[6,16384]{1,0:T(8,128)(2,1)} %scatter.1) | data formatting | bytes 393216
  145.5 0.0 copy-done.1
  (1 shorter events, 0.0 us)
Async XLA Ops:
  0.6 9.0 %copy-start = (bf16[16,16384]{1,0:T(8,128)(2,1)S(1)}, bf16[16,16384]{1,0:T(8,128)(2,1)}, u32[]{:S(2)}) copy-start(bf16[16,16384]{1,0:T(8,128)(2,1)} %param.17) | copy-start | bytes 1572868
  6.0 3.6 %copy-start.2 = (bf16[6,16384]{1,0:T(8,128)(2,1)S(1)}, bf16[6,16384]{1,0:T(8,128)(2,1)}, u32[]{:S(2)}) copy-start(bf16[6,16384]{1,0:T(8,128)(2,1)} %param.11) | copy-start | bytes 589828
  6.0 3.6 %copy-start.3 = (s32[6]{0:T(128)S(1)}, s32[6]{0:T(128)}, u32[]{:S(2)}) copy-start(s32[6]{0:T(128)} %param.16) | copy-start | bytes 76
  39.8 105.7 %copy-start.1 = (bf16[16,16384]{1,0:T(8,128)(2,1)S(1)}, bf16[16,16384]{1,0:T(8,128)(2,1)}, u32[]{:S(2)}) copy-start(bf16[16,16384]{1,0:T(8,128)(2,1)} %param.17) | copy-start | bytes 1572868

commit v3 on v2

--- a/solution.py
+++ b/solution.py
@@ -9,7 +9,7 @@
 from jax.sharding import PartitionSpec as P
 
 LAG = 2
-BACK = 1
+BACK = 2
 VMEM_LIMIT = 66_000_000
 
 

time: 146 us -> 142 us (0.973)
  Pallas kernels: 128 us -> 124 us
    pallas_call x1, Pallas kernels: 78.3 us -> 74.3 us  [per_device(): pl.pallas_call(functools.partial(ffn_kernel, wide, narrow, chunks, ticks)...]
where the time goes in v3:
time: 142 us; the launch traced here: 141 us
  Pallas kernels  124 us (87%)
  local copies, waits for them, and re-layouts  7.1 us (5%)
  matrix products  6.64 us (5%)
  other arithmetic  2.59 us (2%)
    pallas_call x1, Pallas kernels, per_device(): pl.pallas_call(functools.partial(ffn_kernel, wide, narrow, chunks, ticks)...  74.3 us
    pallas_call x1, Pallas kernels, per_device(): pl.pallas_call(functools.partial(scatter_kernel, wide, narrow), out_shape...  25.4 us
    pallas_call x1, Pallas kernels, per_device(): pl.pallas_call(functools.partial(gather_kernel, wide, narrow), out_shape=...  24.5 us
    reshape x1, local copies, waits for them, and re-layouts, per_device(): piece = gathered.reshape(rows, depth)  3.71 us
    dot_general x1, matrix products, per_device(): jnp.einsum('bkgl,bkld->bkgd', probs, values, preferred_element_type=jnp.f...  3.3 us

profile of v3, /device:TPU:0, one launch (start us, length us, event | category | flops | bytes accessed | tf_op | source)
XLA Modules:
  0.0 141.2 jit_solution(6826976580240843294)
XLA Ops:
  0.6 0.0 copy-start
  0.6 0.8 iota_compare_fusion
  1.4 0.8 convert_element_type.19
  2.2 1.0 copy.14
  3.2 2.8 %fusion.3 = f32[6,8,16,256]{3,2,1,0:T(8,128)S(1)} fusion(bf16[6,8,16,128]{3,2,1,0:T(8,128)(2,1)S(1)} %bitcast.26, bf16[6,8,256,128]{3,2,1,0:T(8,128)(2,1)} %param.13, pred[6,256]{1,0:T(8,128)(4,1)S(1)} %iota_compare_fusion), kind=kOutput, calls=%fused_computation.5 | convolution fusion | flops 50724864 | bytes 4130304 | tf_op jit(solution)/shard_map/bkgd,bkld->bkgl/dot_general | solution.py:415
  6.0 0.0 copy-start.2
  6.0 0.0 copy-start.3
  6.0 0.3 fusion.9
  6.3 3.3 %fusion.4 = f32[6,8,16,128]{3,2,1,0:T(8,128)S(1)} fusion(bf16[6,8,256,128]{3,2,1,0:T(8,128)(2,1)} %param.14, f32[6,8,16]{2,1,0:T(8,128)S(1)} %fusion.9, f32[6,8,16,256]{3,2,1,0:T(8,128)S(1)} %fusion.3), kind=kOutput, calls=%fused_computation.10 | convolution fusion | flops 50922496 | bytes 4328448 | tf_op jit(solution)/shard_map/bkgl,bkld->bkgd/dot_general | solution.py:423
  9.6 0.0 copy-done
  9.6 0.0 copy-done.2
  9.6 0.0 copy-done.3
  9.6 0.5 multiply_reduce_fusion
  10.2 0.8 fusion.6
  10.9 0.7 copy.13
  11.6 24.5 %gather.1 = bf16[8,4,192,128]{3,2,1,0:T(8,128)(2,1)} custom-call(bf16[4,192,128]{2,1,0:T(8,128)(2,1)} %bitcast.27), custom_call_target="tpu_custom_call" | custom-call | tf_op jit(solution)/shard_map/gather/pallas_call | solution.py:450
  36.1 3.7 %reshape.52.piece_ref = bf16[192,4096]{1,0:T(8,128)(2,1)} reshape(bf16[8,4,192,128]{3,2,1,0:T(8,128)(2,1)} %gather.1) | data formatting | bytes 3145728 | tf_op jit(solution)/shard_map/reshape | solution.py:468
  39.8 0.0 copy-start.1
  39.8 74.3 %ffn.1 = (f32[4,192,512]{2,1,0:T(8,128)}, bf16[4,192,512]{2,1,0:T(8,128)(2,1)}) custom-call(bf16[192,4096]{1,0:T(8,128)(2,1)} %reshape.52.piece_ref, bf16[4096,3584]{1,0:T(8,128)(2,1)} %gate_ref.1, bf16[4096,3584]{1,0:T(8,128)(2,1)} %up_ref.1, bf16[3584,4096]{1,0:T(8,128)(2,1)} %down_ref.1), custom_call_target="tpu_custom_call" | custom-call | tf_op jit(solution)/shard_map/ffn/pallas_call | solution.py:477
  114.1 25.4 %scatter.1 = bf16[6,16384]{1,0:T(8,128)(2,1)} custom-call(f32[4,192,512]{2,1,0:T(8,128)} %get-tuple-element.4.keep_ref, bf16[4,192,512]{2,1,0:T(8,128)(2,1)} %get-tuple-element.5.give_ref), custom_call_target="tpu_custom_call" | custom-call | tf_op jit(solution)/shard_map/scatter/pallas_call | solution.py:511
  139.5 1.7 %copy.20 = bf16[6,16384]{1,0:T(8,128)(2,1)} copy(bf16[6,16384]{1,0:T(8,128)(2,1)} %scatter.1) | data formatting | bytes 393216
  141.2 0.0 copy-done.1
  (1 shorter events, 0.0 us)
Async XLA Ops:
  0.6 9.0 %copy-start = (bf16[16,16384]{1,0:T(8,128)(2,1)S(1)}, bf16[16,16384]{1,0:T(8,128)(2,1)}, u32[]{:S(2)}) copy-start(bf16[16,16384]{1,0:T(8,128)(2,1)} %param.17) | copy-start | bytes 1572868
  6.0 3.6 %copy-start.2 = (bf16[6,16384]{1,0:T(8,128)(2,1)S(1)}, bf16[6,16384]{1,0:T(8,128)(2,1)}, u32[]{:S(2)}) copy-start(bf16[6,16384]{1,0:T(8,128)(2,1)} %param.11) | copy-start | bytes 589828
  6.0 3.6 %copy-start.3 = (s32[6]{0:T(128)S(1)}, s32[6]{0:T(128)}, u32[]{:S(2)}) copy-start(s32[6]{0:T(128)} %param.16) | copy-start | bytes 76
  39.8 101.4 %copy-start.1 = (bf16[16,16384]{1,0:T(8,128)(2,1)S(1)}, bf16[16,16384]{1,0:T(8,128)(2,1)}, u32[]{:S(2)}) copy-start(bf16[16,16384]{1,0:T(8,128)(2,1)} %param.17) | copy-start | bytes 1572868
